TPU v7x, 32 devices: a whole 2x2x4 slice. The times are simulated.
32 devices in a mesh: seq: 8 (over y, x, core), tensor: 4 (over z).
Axes of the slice: x: 2, y: 2, z: 4, core: 2. Of those that a mesh axis runs over, the one named last changes fastest.
Arguments:
- tokens: bfloat16 [1024, 16384], P('seq', 'tensor'), may hold values from -100 to 100
- norm_gain: float32 [16384], P('tensor'), may hold values from 0.5 to 1.5
- projection_weight: bfloat16 [2048, 16384], P('tensor', 'seq'), may hold values from -1.5 to 1.5
- panel_index: int32 [1], replicated, may hold values from 0 to 31
Outputs:
- gram: float32 [16384, 16384], P('seq', 'tensor')
- factor_panel: bfloat16 [16384, 512], P('seq')
- projected: float32 [2048, 512], P('tensor', 'seq')
All inputs are finite; a program needn't handle non-finite values.
Results may differ from a plain program's by a relative error of at most 0.0057.
Values may be sent and summed in bfloat16 or wider, within the bound.
No kernel may reach another device: no remote copies, remote signals or barrier semaphores. Data moves between devices by JAX's collectives and lax.ppermute only.
A program may use at most 128 MiB of HBM per device.

v0:
```python
import jax
import jax.numpy as jnp
from jax import lax
from jax.sharding import PartitionSpec as P

D = 16384
PANEL = 512
epsilon = 1e-05
damping = 0.1


def broadcast(value, axis, source):
    kept = jnp.where(lax.axis_index(axis) == source, value, 0).astype(value.dtype)
    return lax.psum(kept, axis)


def on_device(tokens, norm_gain, projection_weight, panel_index):
    token_values = tokens.astype(jnp.float32)
    squares = lax.psum(jnp.sum(token_values * token_values, axis=1), "tensor")
    scaled = token_values * lax.rsqrt(squares / D + epsilon)[:, None] * norm_gain[None, :]
    normed = scaled.astype(jnp.bfloat16)
    column_width = normed.shape[1]
    row_width = column_width * lax.axis_size("tensor") // lax.axis_size("seq")
    blocks = column_width // row_width
    seq_index = lax.axis_index("seq")
    tensor_index = lax.axis_index("tensor")
    columns = lax.all_gather(normed, "seq", axis=0, tiled=True)
    local_rows = lax.dynamic_slice_in_dim(columns, seq_index % blocks * row_width, row_width, 1)
    row_part = broadcast(local_rows, "tensor", seq_index // blocks)
    tokens_all = columns.shape[0]
    gram_tile = (
        lax.dot_general(
            row_part, columns, (((0,), (0,)), ((), ())), preferred_element_type=jnp.float32
        )
        / tokens_all
    )
    normed_wide = normed.astype(jnp.float32)
    trace_sum = lax.psum(jnp.sum(normed_wide * normed_wide), ("seq", "tensor")) / tokens_all
    diag_shift = damping * trace_sum / D
    row_ids = seq_index * row_width + lax.iota(jnp.int32, row_width)
    col_ids = tensor_index * column_width + lax.iota(jnp.int32, column_width)
    shifted = gram_tile + jnp.where(
        row_ids[:, None] == col_ids[None, :], diag_shift, jnp.float32(0.0)
    )
    panel_start = panel_index[0] * PANEL
    owner_column = panel_start // column_width
    offset = panel_start - owner_column * column_width
    panel_rows = lax.dynamic_slice_in_dim(shifted, offset, PANEL, 1)
    panel_tokens = lax.dynamic_slice_in_dim(columns, offset, PANEL, 1)
    diag_block = (
        lax.dot_general(
            panel_tokens, panel_tokens, (((0,), (0,)), ((), ())), preferred_element_type=jnp.float32
        )
        / tokens_all
    )
    panel_ids = lax.iota(jnp.int32, PANEL)
    diag_block = diag_block + jnp.where(
        panel_ids[:, None] == panel_ids[None, :], diag_shift, jnp.float32(0.0)
    )
    identity = jnp.eye(PANEL, dtype=jnp.float32)
    diag_block = jnp.where(tensor_index == owner_column, diag_block, identity)
    factor = jnp.linalg.cholesky(diag_block)
    solved = lax.linalg.triangular_solve(
        factor, panel_rows, left_side=False, lower=True, transpose_a=True
    )
    whitened_rows = solved.astype(jnp.bfloat16)
    whitened_full = broadcast(whitened_rows, "tensor", owner_column)
    partial_value = jnp.dot(projection_weight, whitened_full, preferred_element_type=jnp.float32)
    projected = lax.psum_scatter(partial_value, "seq", scatter_dimension=1, tiled=True)
    return (shifted, whitened_full, projected)


def solution(mesh):
    placed = (P("seq", "tensor"), P("tensor"), P("tensor", "seq"), P())
    return jax.shard_map(
        on_device,
        mesh=mesh,
        in_specs=placed,
        out_specs=(P("seq", "tensor"), P("seq", None), P("tensor", "seq")),
        check_vma=False,
    )
```

profile of v0, /device:TPU:0, one launch (start us, length us, event | category | flops | bytes accessed | tf_op | source)
XLA Modules:
  0.0 426.1 jit_solution(7215072890339092447)
XLA Ops:
  7.2 1.7 fusion.9
  8.9 13.5 %psum.28 = f32[128]{0:T(128)S(1)} all-reduce(f32[128]{0:T(128)S(1)} %fusion.9), channel_id=1, replica_groups=mesh['seq'=8,'tensor'=4] {'tensor'}, use_global_device_ids=true, to_apply=%region_1.0 | all-reduce | flops 128 | bytes 1024 | tf_op jit(solution)/shard_map/psum | solution.py:19
  22.4 3.2 multiply_reduce_fusion
  25.7 39.0 %psum.30 = f32[]{:T(128)} all-reduce(f32[]{:T(128)} %get-tuple-element.26), channel_id=1, replica_groups=mesh['seq'=8,'tensor'=4] {'seq','tensor'}, use_global_device_ids=true, to_apply=%region_4.5 | all-reduce | flops 1 | bytes 8 | tf_op jit(solution)/shard_map/psum | solution.py:38
  67.2 11.8 %all-gather.2.cloned.1.call-done = bf16[1024,4096]{1,0:T(8,128)(2,1)} async-done(((bf16[128,4096]{1,0:T(8,128)(2,1)}), bf16[1024,4096]{1,0:T(8,128)(2,1)}) %all-gather.2.cloned.1.call-update) | async-done | bytes 8388624 | tf_op jit(solution)/shard_map/all_gather | solution.py:27
  79.0 5.5 %dynamic-slice_select_fusion = bf16[1024,2048]{1,0:T(8,128)(2,1)} fusion(bf16[1024,4096]{1,0:T(8,128)(2,1)} %all-gather.2.cloned.1.call-done, s32[]{:T(128)S(6)} %select_n.66, pred[]{:T(512)S(6)} %eq.56), kind=kLoop, calls=%fused_computation.3 | loop fusion | flops 2097152 | bytes 8388613 | tf_op jit(solution)/shard_map/jit(_where)/select_n | solution.py:13
  85.2 3.7 convert_select_fusion
  88.9 1.6 copy.11
  90.5 1.6 fusion.19
  92.1 1.0 copy-done.1
  93.0 11.7 %cholesky.103 = f32[128,128]{1,0:T(8,128)S(1)} custom-call(f32[128,128]{1,0:T(8,128)S(1)} %cholesky.263), custom_call_target="Cholesky" | custom-call | tf_op jit(solution)/shard_map/jit(cholesky)/cholesky | solution.py:62
  105.3 9.8 %custom-call.30 = f32[1,128,128]{1,2,0:T(8,128)S(1)} custom-call(f32[1,128,128]{2,1,0:T(8,128)S(1)} %get-tuple-element.35), custom_call_target="InvertDiagBlocksLowerTriangular" | custom-call | tf_op jit(solution)/shard_map/jit(cholesky)/cholesky | solution.py:62
  115.1 1.2 fusion.24
  116.4 1.3 convolution_subtract_fusion.2
  117.7 0.7 copy.12
  118.5 11.7 %cholesky.215 = f32[128,128]{1,0:T(8,128)S(1)} custom-call(f32[128,128]{1,0:T(8,128)S(1)} %cholesky.267), custom_call_target="Cholesky" | custom-call | tf_op jit(solution)/shard_map/jit(cholesky)/cholesky | solution.py:62
  130.2 0.7 copy.14
  131.5 10.6 %custom-call.31 = f32[1,128,128]{1,2,0:T(8,128)} custom-call(f32[1,128,128]{2,1,0:T(8,128)S(1)} %get-tuple-element.33), custom_call_target="InvertDiagBlocksLowerTriangular" | custom-call | tf_op jit(solution)/shard_map/jit(cholesky)/cholesky | solution.py:62
  142.0 1.0 cholesky.222
  143.0 0.8 constant_dynamic-update-slice_fusion.3
  143.9 1.2 convolution_dynamic-update-slice_fusion
  145.0 1.5 convolution_subtract_fusion.3
  146.6 11.7 %cholesky.236 = f32[128,128]{1,0:T(8,128)S(1)} custom-call(f32[128,128]{1,0:T(8,128)S(1)} %cholesky.272), custom_call_target="Cholesky" | custom-call | tf_op jit(solution)/shard_map/jit(cholesky)/cholesky | solution.py:62
  158.4 9.8 %custom-call.32 = f32[1,128,128]{1,2,0:T(8,128)S(1)} custom-call(f32[1,128,128]{2,1,0:T(8,128)S(1)} %get-tuple-element.31), custom_call_target="InvertDiagBlocksLowerTriangular" | custom-call | tf_op jit(solution)/shard_map/jit(cholesky)/cholesky | solution.py:62
  168.5 1.3 convolution_subtract_fusion.4
  169.9 11.9 %cholesky.253 = f32[128,128]{1,0:T(8,128)S(1)} custom-call(f32[128,128]{1,0:T(8,128)S(1)} %convolution_subtract_fusion.4), custom_call_target="Cholesky" | custom-call | tf_op jit(solution)/shard_map/jit(cholesky)/cholesky | solution.py:62
  181.9 1.3 compare_reduce_fusion.2
  187.1 1.1 select_select_fusion
  188.2 0.7 triangular_solve.90
  188.9 14.3 %while.1 = (s32[]{:T(128)}, f32[512,512]{0,1:T(8,128)}, s32[4,2]{0,1:T(2,128)S(1)}, f32[4,128,128]{2,1,0:T(8,128)}, s32[]{:T(128)}) while((s32[]{:T(128)}, f32[512,512]{0,1:T(8,128)}, s32[4,2]{0,1:T(2,128)S(1)}, f32[4,128,128]{2,1,0:T(8,128)}, s32[]{:T(128)}) %tuple.34), condition=%wide.while_cond, body=%wide.while_body.sunk | while | flops 2 | bytes 393329 | solution.py:63
  189.5 2.3 dynamic-slice.18
  193.1 2.3 dynamic-slice.18
  196.7 2.3 dynamic-slice.18
  200.3 2.2 dynamic-slice.18
  203.2 40.1 %custom-call.33 = f32[4,128,128]{1,2,0:T(8,128)S(1)} custom-call(f32[4,128,128]{2,1,0:T(8,128)} %get-tuple-element.10), custom_call_target="InvertDiagBlocksLowerTriangular" | custom-call | tf_op jit(solution)/shard_map/triangular_solve | solution.py:63
  243.3 28.2 %select_add_fusion = f32[2048,4096]{1,0:T(8,128)} fusion(bf16[1024,2048]{1,0:T(8,128)(2,1)} %all-reduce.4.cloned.1.call-done, bf16[1024,4096]{1,0:T(8,128)(2,1)} %all-gather.2.cloned.1.call-done, f32[]{:T(128)S(6)} %div.54, s32[4096]{0:T(1024)S(1)} %iota_add_fusion, s32[2048]{0:T(1024)} %iota_add_fusion.1), kind=kOutput, calls=%fused_computation.2 | convolution fusion | flops 17213423616 | bytes 46161924 | tf_op jit(solution)/shard_map/dot_general | solution.py:32
  271.6 2.3 fusion.45
  273.9 3.1 convolution_subtract_fusion.1
  277.0 1.1 fusion.44
  278.1 5.0 %convolution_subtract_fusion = f32[2048,128]{1,0:T(8,128)S(1)} fusion(f32[2048,128]{0,1:T(8,128)S(1)} %get-tuple-element.41, f32[2048,128]{0,1:T(8,128)S(1)} %get-tuple-element.43, f32[2048,4096]{1,0:T(8,128)} %select_add_fusion, s32[]{:T(128)S(6)} %add.113, f32[512,512]{0,1:T(8,128)} %get-tuple-element.100), kind=kOutput, calls=%fused_computation.13 | convolution fusion | flops 806092800 | bytes 4325380 | tf_op jit(solution)/shard_map/triangular_solve | solution.py:63
  283.0 1.1 fusion.43
  284.1 6.9 %fusion.6 = f32[2048,128]{1,0:T(8,128)S(1)} fusion(f32[2048,128]{0,1:T(8,128)S(1)} %get-tuple-element.39, f32[2048,128]{0,1:T(8,128)S(1)} %get-tuple-element.41, f32[2048,128]{0,1:T(8,128)S(1)} %get-tuple-element.43, f32[2048,4096]{1,0:T(8,128)} %select_add_fusion, s32[]{:T(128)S(6)} %add.114, f32[512,512]{0,1:T(8,128)} %get-tuple-element.100), kind=kOutput, calls=%fused_computation.12 | convolution fusion | flops 1209794560 | bytes 5439492 | tf_op jit(solution)/shard_map/triangular_solve | solution.py:63
  291.0 1.1 convolution_convert_fusion
  292.1 1.9 maximum_select_fusion
  294.0 86.3 %all-reduce.6.cloned.1.call-done = bf16[2048,512]{0,1:T(8,128)(2,1)} async-done(((bf16[2048,512]{0,1:T(8,128)(2,1)}), bf16[2048,512]{0,1:T(8,128)(2,1)}) %all-reduce.6.cloned.1.call-update) | async-done | bytes 2097168 | tf_op jit(solution)/shard_map/psum | solution.py:14
  380.3 3.9 convolution_bitcast_fusion
  384.2 3.9 copy.20
  388.1 31.2 %reduce-scatter.2.cloned.1.call-done = f32[512,64]{0,1:T(8,128)} async-done(((f32[512,512]{0,1:T(8,128)}), f32[512,64]{0,1:T(8,128)}) %reduce-scatter.2.cloned.1.call-update) | async-done | bytes 131088 | tf_op jit(solution)/shard_map/reduce_scatter | solution.py:69
  (49 shorter events, 10.4 us)
Async XLA Ops:
  7.2 373.2 %copy-start = (bf16[512,2048]{1,0:T(8,128)(2,1)S(1)}, bf16[512,2048]{1,0:T(8,128)(2,1)}, u32[]{:S(2)}) copy-start(bf16[512,2048]{1,0:T(8,128)(2,1)} %param.6) | copy-start | bytes 6291460
  7.2 71.9 %all-gather.2.cloned.1.call-start = ((), (), s32[]{:S(2)}) async-start(), calls=%async_computation.1 | async-start | bytes 9437184 | tf_op jit(solution)/shard_map/all_gather | solution.py:27
  25.6 217.7 %all-reduce.4.cloned.1.call-start = ((), (), s32[]{:S(2)}) async-start(), calls=%async_computation.2 | async-start | bytes 8388608 | tf_op jit(solution)/shard_map/psum | solution.py:14
  84.6 295.7 %all-reduce.6.cloned.1.call-start = ((), (), s32[]{:S(2)}) async-start(), calls=%async_computation.3 | async-start | bytes 4194304 | tf_op jit(solution)/shard_map/psum | solution.py:14
  92.1 1.0 copy-start.1
  294.0 125.4 %reduce-scatter.2.cloned.1.call-start = ((), (), s32[]{:S(2)}) async-start(), calls=%async_computation.4 | async-start | bytes 1179648 | tf_op jit(solution)/shard_map/reduce_scatter | solution.py:69
Sparse Core Ops, SparseCore 0:
  25.8 53.2 all-gather.1
  84.7 155.1 all-reduce.3
  294.1 86.1 all-reduce.5
  384.3 35.0 reduce-scatter.1
where the time goes:
time: 430 us; the launch traced here: 426 us
  other arithmetic  137 us (32%)
  waiting for transfers between devices  129 us (30%)
  matrix products  63 us (15%)
  blocking collectives  52.4 us (12%)
  local copies, waits for them, and re-layouts  25.1 us (6%)
  between operations  18.2 us (4%)
    psum x2, waiting for transfers between devices, broadcast(): return lax.psum(kept, axis)  86.3 us
    another operation x14, other arithmetic, on_device(): factor = jnp.linalg.cholesky(diag_block)  80.9 us
    another operation x3, other arithmetic, on_device(): lax.linalg.triangular_solve(factor, panel_rows, left_side=False, lower=Tr...  41.8 us
    psum x1, blocking collectives, on_device(): lax.psum(jnp.sum(normed_wide * normed_wide), ('seq', 'tensor')) / tokens_all  39 us
    reduce_scatter x1, waiting for transfers between devices, on_device(): lax.psum_scatter(partial_value, 'seq', scatter_dimension=1, tiled=True)  31.2 us
    dot_general x1, matrix products, on_device(): lax.dot_general(row_part, columns, (((0,), (0,)), ((), ())), preferred_el...  28.2 us
    another operation x7, matrix products, on_device(): lax.linalg.triangular_solve(factor, panel_rows, left_side=False, lower=Tr...  20.5 us
    another operation x20, local copies, waits for them, and re-layouts  14.3 us
  transfers between devices with their start and end apart: 4, of which 3 were waited for; matrix products, arithmetic and copies ran while one was open for 37% of the time, Pallas kernels for 0%

commit v1 on v0

--- a/solution.py
+++ b/solution.py
@@ -11,7 +11,7 @@
 
 def broadcast(value, axis, source):
     kept = jnp.where(lax.axis_index(axis) == source, value, 0).astype(value.dtype)
-    return lax.psum(kept, axis)
+    return jnp.sum(lax.all_gather(kept, axis), axis=0)
 
 
 def on_device(tokens, norm_gain, projection_weight, panel_index):

time: 430 us -> 642 us (1.49)
  waiting for transfers between devices: 129 us -> 310 us
  other arithmetic: 137 us -> 156 us
  blocking collectives: 52.4 us -> 65 us
    all_gather x0 -> x2, waiting for transfers between devices: none -> 223 us  [broadcast(): return jnp.sum(lax.all_gather(kept, axis), axis=0)]
    psum x2 -> x0, waiting for transfers between devices: 86.3 us -> none  [broadcast(): return lax.psum(kept, axis)]
    all_gather x1, waiting for transfers between devices: 11.8 us -> 52.5 us  [on_device(): columns = lax.all_gather(normed, 'seq', axis=0, tiled=True)]
    psum x1, blocking collectives: 39 us -> 51.6 us  [on_device(): lax.psum(jnp.sum(normed_wide * normed_wide), ('seq', 'tensor')) / tokens_all]
    reduce_sum x0 -> x1, other arithmetic: none -> 12.1 us  [broadcast(): return jnp.sum(lax.all_gather(kept, axis), axis=0)]
    unnamed x1 -> x2, other arithmetic: 0.01 us -> 6.63 us
    another operation x3 -> x6, other arithmetic: 41.8 us -> 42 us  [on_device(): lax.linalg.triangular_solve(factor, panel_rows, left_side=False, lower=Tr...]
  transfers between devices with their start and end apart: 4 -> 4, of which waited for: 3 -> 4; matrix products, arithmetic and copies ran while one was open for 37% -> 24% of each run, Pallas kernels for 0% -> 0%
where the time goes in v1:
time: 642 us; the launch traced here: 638 us
  waiting for transfers between devices  310 us (48%)
  other arithmetic  156 us (24%)
  blocking collectives  65 us (10%)
  matrix products  62.9 us (10%)
  local copies, waits for them, and re-layouts  25 us (4%)
  between operations  18.2 us (3%)
    all_gather x2, waiting for transfers between devices, broadcast(): return jnp.sum(lax.all_gather(kept, axis), axis=0)  223 us
    another operation x14, other arithmetic, on_device(): factor = jnp.linalg.cholesky(diag_block)  81.3 us
    all_gather x1, waiting for transfers between devices, on_device(): columns = lax.all_gather(normed, 'seq', axis=0, tiled=True)  52.5 us
    psum x1, blocking collectives, on_device(): lax.psum(jnp.sum(normed_wide * normed_wide), ('seq', 'tensor')) / tokens_all  51.6 us
    another operation x6, other arithmetic, on_device(): lax.linalg.triangular_solve(factor, panel_rows, left_side=False, lower=Tr...  42 us
    reduce_scatter x1, waiting for transfers between devices, on_device(): lax.psum_scatter(partial_value, 'seq', scatter_dimension=1, tiled=True)  34.3 us
    dot_general x1, matrix products, on_device(): lax.dot_general(row_part, columns, (((0,), (0,)), ((), ())), preferred_el...  27.9 us
    another operation x7, matrix products, on_device(): lax.linalg.triangular_solve(factor, panel_rows, left_side=False, lower=Tr...  20.5 us
  transfers between devices with their start and end apart: 4, of which 4 were waited for; matrix products, arithmetic and copies ran while one was open for 24% of the time, Pallas kernels for 0%

profile of v1, /device:TPU:0, one launch (start us, length us, event | category | flops | bytes accessed | tf_op | source)
XLA Modules:
  0.0 637.9 jit_solution(15803451828422392584)
XLA Ops:
  7.2 1.7 fusion.10
  8.9 13.5 %psum.14 = f32[128]{0:T(128)S(1)} all-reduce(f32[128]{0:T(128)S(1)} %fusion.10), channel_id=1, replica_groups=mesh['seq'=8,'tensor'=4] {'tensor'}, use_global_device_ids=true, to_apply=%region_1.0 | all-reduce | flops 128 | bytes 1024 | tf_op jit(solution)/shard_map/psum | solution.py:19
  22.4 3.2 multiply_reduce_fusion
  25.7 52.5 %all-gather.5.cloned.1.call-done = bf16[1024,4096]{1,0:T(8,128)(2,1)} async-done(((bf16[128,4096]{1,0:T(8,128)(2,1)}), bf16[1024,4096]{1,0:T(8,128)(2,1)}) %all-gather.5.cloned.1.call-update) | async-done | bytes 8388624 | tf_op jit(solution)/shard_map/all_gather | solution.py:27
  78.3 5.5 dynamic-slice_select_fusion
  83.8 51.6 %psum.15 = f32[]{:T(128)} all-reduce(f32[]{:T(128)} %get-tuple-element.30), channel_id=1, replica_groups=mesh['seq'=8,'tensor'=4] {'seq','tensor'}, use_global_device_ids=true, to_apply=%region_4.5 | all-reduce | flops 1 | bytes 8 | tf_op jit(solution)/shard_map/psum | solution.py:38
  138.0 3.7 convert_select_fusion
  141.7 1.6 copy.24
  143.3 1.5 fusion.20
  144.7 1.0 copy-done.1
  145.7 11.7 %cholesky.103 = f32[128,128]{1,0:T(8,128)S(1)} custom-call(f32[128,128]{1,0:T(8,128)S(1)} %cholesky.263), custom_call_target="Cholesky" | custom-call | tf_op jit(solution)/shard_map/jit(cholesky)/cholesky | solution.py:62
  158.8 9.8 %custom-call.30 = f32[1,128,128]{1,2,0:T(8,128)S(1)} custom-call(f32[1,128,128]{2,1,0:T(8,128)S(1)} %get-tuple-element.39), custom_call_target="InvertDiagBlocksLowerTriangular" | custom-call | tf_op jit(solution)/shard_map/jit(cholesky)/cholesky | solution.py:62
  168.6 1.2 fusion.25
  169.9 1.3 convolution_subtract_fusion.2
  171.2 11.7 %cholesky.215 = f32[128,128]{1,0:T(8,128)S(1)} custom-call(f32[128,128]{1,0:T(8,128)S(1)} %cholesky.267), custom_call_target="Cholesky" | custom-call | tf_op jit(solution)/shard_map/jit(cholesky)/cholesky | solution.py:62
  184.3 10.6 %custom-call.31 = f32[1,128,128]{1,2,0:T(8,128)} custom-call(f32[1,128,128]{2,1,0:T(8,128)S(1)} %get-tuple-element.37), custom_call_target="InvertDiagBlocksLowerTriangular" | custom-call | tf_op jit(solution)/shard_map/jit(cholesky)/cholesky | solution.py:62
  194.9 1.0 cholesky.222
  195.9 0.8 constant_dynamic-update-slice_fusion.3
  196.7 1.2 convolution_dynamic-update-slice_fusion
  197.9 1.5 convolution_subtract_fusion.3
  199.4 11.7 %cholesky.236 = f32[128,128]{1,0:T(8,128)S(1)} custom-call(f32[128,128]{1,0:T(8,128)S(1)} %cholesky.272), custom_call_target="Cholesky" | custom-call | tf_op jit(solution)/shard_map/jit(cholesky)/cholesky | solution.py:62
  211.3 9.8 %custom-call.32 = f32[1,128,128]{1,2,0:T(8,128)S(1)} custom-call(f32[1,128,128]{2,1,0:T(8,128)S(1)} %get-tuple-element.35), custom_call_target="InvertDiagBlocksLowerTriangular" | custom-call | tf_op jit(solution)/shard_map/jit(cholesky)/cholesky | solution.py:62
  221.4 1.3 convolution_subtract_fusion.4
  222.7 12.1 %cholesky.253 = f32[128,128]{1,0:T(8,128)S(1)} custom-call(f32[128,128]{1,0:T(8,128)S(1)} %convolution_subtract_fusion.4), custom_call_target="Cholesky" | custom-call | tf_op jit(solution)/shard_map/jit(cholesky)/cholesky | solution.py:62
  234.9 1.3 compare_reduce_fusion.2
  240.2 1.1 select_select_fusion
  242.0 14.3 %while.1 = (s32[]{:T(128)}, f32[512,512]{0,1:T(8,128)}, s32[4,2]{0,1:T(2,128)S(1)}, f32[4,128,128]{2,1,0:T(8,128)}, s32[]{:T(128)}) while((s32[]{:T(128)}, f32[512,512]{0,1:T(8,128)}, s32[4,2]{0,1:T(2,128)S(1)}, f32[4,128,128]{2,1,0:T(8,128)}, s32[]{:T(128)}) %tuple.32), condition=%wide.while_cond, body=%wide.while_body.sunk | while | flops 2 | bytes 393329 | solution.py:63
  242.6 2.3 dynamic-slice.16
  246.2 2.3 dynamic-slice.16
  249.8 2.3 dynamic-slice.16
  253.4 2.2 dynamic-slice.16
  256.3 40.1 %custom-call.33 = f32[4,128,128]{1,2,0:T(8,128)S(1)} custom-call(f32[4,128,128]{2,1,0:T(8,128)} %get-tuple-element.10), custom_call_target="InvertDiagBlocksLowerTriangular" | custom-call | tf_op jit(solution)/shard_map/triangular_solve | solution.py:63
  296.4 75.3 %all-gather.9.cloned.1.call-done = bf16[4096,2048]{1,0:T(8,128)(2,1)} async-done(((bf16[1024,2048]{1,0:T(8,128)(2,1)}), bf16[4096,2048]{1,0:T(8,128)(2,1)}) %all-gather.9.cloned.1.call-update) | async-done | bytes 16777232 | tf_op jit(solution)/shard_map/all_gather | solution.py:14
  371.7 12.1 %reduce_sum.43 = bf16[1024,2048]{1,0:T(8,128)(2,1)} reduce(bf16[4,1024,2048]{2,1,0:T(8,128)(2,1)} %bitcast.66, bf16[]{:T(256)} %constant.204.clone.1), dimensions={0}, to_apply=%region_2.3 | reduce | flops 6291456 | bytes 20971522 | tf_op jit(solution)/shard_map/reduce_sum | solution.py:14
  383.8 27.9 %select_add_fusion = f32[2048,4096]{1,0:T(8,128)} fusion(bf16[1024,2048]{1,0:T(8,128)(2,1)} %reduce_sum.43, bf16[1024,4096]{1,0:T(8,128)(2,1)} %all-gather.5.cloned.1.call-done, f32[]{:T(128)S(6)} %div.54, s32[4096]{0:T(1024)S(1)} %iota_add_fusion, s32[2048]{0:T(1024)S(1)} %copy-done.2), kind=kOutput, calls=%fused_computation.2 | convolution fusion | flops 17213423616 | bytes 46161924 | tf_op jit(solution)/shard_map/dot_general | solution.py:32
  411.7 2.3 fusion.16
  414.1 3.1 convolution_subtract_fusion.1
  417.2 1.1 fusion.31
  418.4 5.0 convolution_subtract_fusion
  423.4 1.1 fusion.30
  424.5 6.9 %fusion.6 = f32[2048,128]{1,0:T(8,128)S(1)} fusion(f32[2048,128]{0,1:T(8,128)S(1)} %fusion.30, f32[2048,128]{0,1:T(8,128)S(1)} %fusion.31, f32[2048,128]{0,1:T(8,128)S(1)} %fusion.16, f32[2048,4096]{1,0:T(8,128)} %select_add_fusion, s32[]{:T(128)S(6)} %add.110, f32[512,512]{0,1:T(8,128)} %get-tuple-element.100), kind=kOutput, calls=%fused_computation.12 | convolution fusion | flops 1209794560 | bytes 5439492 | tf_op jit(solution)/shard_map/triangular_solve | solution.py:63
  431.4 1.1 fusion.9
  432.5 1.9 maximum_select_fusion
  434.4 3.9 copy.33
  438.4 147.9 %all-gather.7.cloned.1.call-done = bf16[4,2048,512]{2,1,0:T(8,128)(2,1)} async-done(((bf16[1,2048,512]{2,1,0:T(8,128)(2,1)}), bf16[4,2048,512]{2,1,0:T(8,128)(2,1)}) %all-gather.7.cloned.1.call-update) | async-done | bytes 8388624 | tf_op jit(solution)/shard_map/all_gather | solution.py:14
  586.3 6.6 %reduce_sum.45 = bf16[2048,512]{1,0:T(8,128)(2,1)} reduce(bf16[4,2048,512]{2,1,0:T(8,128)(2,1)} %all-gather.7.cloned.1.call-done, bf16[]{:T(256)} %constant.204.clone.1), dimensions={0}, to_apply=%region_13.14 | reduce | flops 3145728 | bytes 10485762
  592.9 3.9 convolution_bitcast_fusion
  596.8 34.3 %reduce-scatter.2.cloned.1.call-done = f32[512,64]{0,1:T(8,128)} async-done(((f32[512,512]{0,1:T(8,128)}), f32[512,64]{0,1:T(8,128)}) %reduce-scatter.2.cloned.1.call-update) | async-done | bytes 131088 | tf_op jit(solution)/shard_map/reduce_scatter | solution.py:69
  (56 shorter events, 12.3 us)
Async XLA Ops:
  7.2 585.8 %copy-start = (bf16[512,2048]{1,0:T(8,128)(2,1)S(1)}, bf16[512,2048]{1,0:T(8,128)(2,1)}, u32[]{:S(2)}) copy-start(bf16[512,2048]{1,0:T(8,128)(2,1)} %param.6) | copy-start | bytes 6291460
  7.2 71.1 %all-gather.5.cloned.1.call-start = ((), (), s32[]{:S(2)}) async-start(), calls=%async_computation.1 | async-start | bytes 9437184 | tf_op jit(solution)/shard_map/all_gather | solution.py:27
  25.6 346.1 %all-gather.9.cloned.1.call-start = ((), (), s32[]{:S(2)}) async-start(), calls=%async_computation.4 | async-start | bytes 20971520 | tf_op jit(solution)/shard_map/all_gather | solution.py:14
  83.8 502.5 %all-gather.7.cloned.1.call-start = ((), (), s32[]{:S(2)}) async-start(), calls=%async_computation.2 | async-start | bytes 10485760 | tf_op jit(solution)/shard_map/all_gather | solution.py:14
  144.7 1.0 copy-start.1
  371.7 12.1 %copy-start.2 = (s32[2048]{0:T(1024)S(1)}, s32[2048]{0:T(1024)}, u32[]{:S(2)}) copy-start(s32[2048]{0:T(1024)} %iota_add_fusion.1) | copy-start | bytes 24580
  438.3 192.8 %reduce-scatter.2.cloned.1.call-start = ((), (), s32[]{:S(2)}) async-start(), calls=%async_computation.3 | async-start | bytes 1179648 | tf_op jit(solution)/shard_map/reduce_scatter | solution.py:69
Sparse Core Ops, SparseCore 0:
  25.8 52.4 all-gather.4
  83.9 287.7 all-gather.8
  438.4 147.7 all-gather.6
  596.9 34.1 reduce-scatter.1
